TPU v7x, 512 devices: a whole 4x8x8 slice. The times are simulated.
512 devices in a mesh: kpt: 8 (over x, core), band: 64 (over y, z).
Axes of the slice: x: 4, y: 8, z: 8, core: 2. Of those that a mesh axis runs over, the one named last changes fastest.
Arguments:
- orbitals: bfloat16 [8, 2, 256, 32768], P('kpt', None, 'band'), may hold values from -6 to 6
- potential: float32 [32768], replicated, may hold values from -3 to -0.5
- kernel: float32 [8, 32768], P('kpt'), may hold values from 0.1 to 4
- owners: int32 [4], replicated, may hold values from 0 to 255, as said below
- partner: int32 [8, 4], replicated, may hold values from 0 to 7, as said below
Outputs:
- residual: bfloat16 [8, 2, 256, 32768], P('kpt', None, 'band')
Inputs may be any that keep to these rules, and one draw needn't show every extreme that they name: `owners`: 4 distinct band indices, among them 0 and 255. `partner`: k-point indices.
All inputs are finite; a program needn't handle non-finite values.
Results may differ from a plain program's by a relative error of at most 0.0075.
Values may be sent and summed in bfloat16 or wider, within the bound.
A program may use at most 128 MiB of HBM per device.

v0:
```python
import jax
import jax.numpy as jnp
from jax import lax
from jax.sharding import PartitionSpec as P

G = 32
GRID = 32768
OWNERS = 4


FRACTION = 0.25
HIGHEST = lax.Precision.HIGHEST


def joined_along(pieces, dim):
    pieces = jnp.moveaxis(pieces, 0, dim)
    lengths = pieces.shape
    return pieces.reshape(*lengths[:dim], lengths[dim] * lengths[dim + 1], *lengths[dim + 2 :])


def copy_for_each(array, axis):
    peers = lax.axis_size(axis)
    return lax.all_to_all(
        jnp.broadcast_to(array[None], (peers, *array.shape)), axis, 0, 0, tiled=True
    )


def collect(array, axis, dim):
    return joined_along(copy_for_each(array, axis), dim)


def rotation(angles, direction):
    cosine = jnp.cos(angles)
    sine_part = jnp.sin(angles) * direction
    upper_row = jnp.stack([cosine, sine_part])
    lower_row = jnp.stack([-sine_part, cosine])
    return jnp.stack([upper_row, lower_row])


def first_angles(outer_count):
    width = G * outer_count
    indices = jnp.arange(width, dtype=jnp.int32)
    frequency = indices // outer_count
    within = indices % outer_count
    fraction = (frequency[:, None] * frequency[None, :] % G).astype(jnp.float32) / G
    fraction = (
        fraction
        + (within[:, None] * within[None, :] % outer_count).astype(jnp.float32) / outer_count
    )
    return fraction * (2.0 * jnp.pi)


def block_angles(outer_count, block_width):
    rows_outer = jnp.arange(outer_count, dtype=jnp.int32)
    out_index = jnp.arange(block_width, dtype=jnp.int32)
    in_index = jnp.arange(block_width, dtype=jnp.int32)
    high_freq = out_index // G
    last_freq = out_index % G
    low_cell = in_index // G
    last_cell = in_index % G
    turning = low_cell[None, None, :] * (
        rows_outer[:, None, None] + outer_count * high_freq[None, :, None]
    )
    fraction = (turning % G).astype(jnp.float32) / G
    fraction = (
        fraction + (last_cell[None, None, :] * last_freq[None, :, None] % G).astype(jnp.float32) / G
    )
    return fraction * (2.0 * jnp.pi)


def exchange_field(resident, phases, kernel_grid):
    inner_count = min(G, max(1, 128 // G))
    outer_count = G // inner_count
    block_width = inner_count * G
    owner_count = phases.shape[0]
    band_re = resident[0].astype(jnp.float32)
    band_im = resident[1].astype(jnp.float32)
    owner_re = phases[:, 0].astype(jnp.float32)
    owner_im = phases[:, 1].astype(jnp.float32)
    density = jnp.stack(
        [
            owner_re[:, None] * band_re[None] + owner_im[:, None] * band_im[None],
            owner_re[:, None] * band_im[None] - owner_im[:, None] * band_re[None],
        ],
        axis=2,
    )
    batch_count = density.shape[0] * density.shape[1]
    plain_angles = first_angles(outer_count)
    inner_angles = block_angles(outer_count, block_width)
    scaled = kernel_grid.reshape(G, inner_count, outer_count, G)
    scaled = jnp.transpose(scaled, (0, 2, 1, 3)).reshape(G, outer_count, block_width) / GRID
    current = density.reshape(batch_count, 2, G * outer_count, block_width)
    current = jnp.einsum("bcpq,dcsp->bdsq", current, rotation(plain_angles, 1.0), precision=HIGHEST)
    current = current.reshape(batch_count, 2, G, outer_count, block_width)
    current = jnp.einsum(
        "bcxhq,dchpq->bdxhp", current, rotation(inner_angles, 1.0), precision=HIGHEST
    )
    current = current * scaled
    current = jnp.einsum(
        "bcxhq,dchpq->bdxhp",
        current,
        rotation(jnp.swapaxes(inner_angles, 1, 2), -1.0),
        precision=HIGHEST,
    )
    current = current.reshape(batch_count, 2, G * outer_count, block_width)
    current = jnp.einsum(
        "bcpq,dcsp->bdsq", current, rotation(plain_angles, -1.0), precision=HIGHEST
    )
    solved = current.reshape(owner_count, resident.shape[1], 2, GRID)
    term_re = jnp.sum(
        owner_re[:, None] * solved[:, :, 0] - owner_im[:, None] * solved[:, :, 1], axis=0
    )
    term_im = jnp.sum(
        owner_re[:, None] * solved[:, :, 1] + owner_im[:, None] * solved[:, :, 0], axis=0
    )
    return -FRACTION * jnp.stack([term_re, term_im])


def combine(over_re, over_im, rows_re, rows_im, proj_re, proj_im):
    mixed_re = jnp.dot(over_re, proj_re, precision=HIGHEST) - jnp.dot(
        over_im, proj_im, precision=HIGHEST
    )
    mixed_im = jnp.dot(over_re, proj_im, precision=HIGHEST) + jnp.dot(
        over_im, proj_re, precision=HIGHEST
    )
    return jnp.stack([2.0 * rows_re - mixed_re, 2.0 * rows_im - mixed_im])


def build_block(coeff):
    real_t = coeff[0].T
    imag_t = coeff[1].T
    upper = jnp.concatenate([real_t, -imag_t], axis=1)
    lower = jnp.concatenate([imag_t, real_t], axis=1)
    return jnp.concatenate([upper, lower], axis=0)


def body(orbitals, potential, kernel, owners, partner):
    resident = orbitals[0]
    band_dev = resident.shape[1]
    band_index = lax.axis_index("band")
    kpoint_index = lax.axis_index("kpt")
    targets = partner[kpoint_index]
    member_ids = jnp.arange(OWNERS, dtype=jnp.int32)
    orbital_slabs = lax.all_to_all(orbitals, "band", split_axis=3, concat_axis=2, tiled=True)
    masked_parts = []
    for member in range(OWNERS):
        target = owners[member]
        chosen = lax.dynamic_index_in_dim(resident, target % band_dev, 1, keepdims=False)
        masked_parts.append(
            jnp.where(target // band_dev == band_index, chosen, jnp.zeros_like(chosen))
        )
    masked = jnp.stack(masked_parts)
    arrived = lax.all_to_all(masked[None], "band", split_axis=3, concat_axis=0, tiled=True)
    shares = jnp.sum(arrived.astype(jnp.float32), axis=0).astype(jnp.bfloat16)
    all_shares = collect(shares[None], "kpt", 0)
    mine_piece = all_shares[targets, member_ids]
    phases = collect(mine_piece, "band", 2)
    exchange = exchange_field(resident, phases, kernel[0])
    values = (potential * resident.astype(jnp.float32) + exchange).astype(jnp.bfloat16)
    value_slabs = lax.all_to_all(values[None], "band", split_axis=3, concat_axis=2, tiled=True)
    slab_own = orbital_slabs[0]
    slab_val = value_slabs[0]
    bands_all = slab_own.shape[1]
    slab_cells = slab_own.shape[2]
    cross_own = jnp.einsum("cig,djg->cidj", slab_own, slab_own, preferred_element_type=jnp.float32)
    cross_val = jnp.einsum("cig,djg->cidj", slab_own, slab_val, preferred_element_type=jnp.float32)
    partial_sums = (
        jnp.stack(
            [
                cross_own[0, :, 0] + cross_own[1, :, 1],
                cross_own[0, :, 1] - cross_own[1, :, 0],
                cross_val[0, :, 0] + cross_val[1, :, 1],
                cross_val[0, :, 1] - cross_val[1, :, 0],
            ]
        )
        / GRID
    )
    totals = lax.psum(partial_sums, "band")
    coeff = combine(totals[0], totals[1], totals[2], totals[3], totals[2], totals[3]).astype(
        jnp.bfloat16
    )
    mixing = build_block(coeff)
    correction = jnp.dot(
        mixing, slab_own.reshape(2 * bands_all, slab_cells), preferred_element_type=jnp.float32
    )
    residual_slab = slab_val.astype(jnp.float32).reshape(2 * bands_all, slab_cells) - correction
    residual_slab = residual_slab.reshape(1, 2, bands_all, slab_cells).astype(jnp.bfloat16)
    return lax.all_to_all(residual_slab, "band", split_axis=2, concat_axis=3, tiled=True)


def solution(mesh):
    in_specs = (P("kpt", None, "band", None), P(), P("kpt", None), P(), P())
    out_specs = P("kpt", None, "band", None)
    return jax.shard_map(body, mesh=mesh, in_specs=in_specs, out_specs=out_specs, check_vma=False)
```

profile of v0, /device:TPU:1, one launch (start us, length us, event | category | flops | bytes accessed | tf_op | source)
XLA Modules:
  0.0 721.0 jit_solution(3806923685248856827)
XLA Ops:
  6.5 1.5 fusion.98
  18.4 2.9 constant_dynamic-slice_fusion.3
  22.2 1.0 maximum_bitcast_fusion.15
  23.1 25.7 %copy.99 = bf16[1,4,2,32768]{1,2,0,3:T(2,128)(2,1)} copy(bf16[1,4,2,32768]{3,2,1,0:T(2,128)(2,1)S(1)} %maximum_bitcast_fusion.15) | data formatting | bytes 1048576 | tf_op jit(solution)/shard_map/broadcast_in_dim | solution.py:153
  48.8 31.9 %reshape.1203 = bf16[64,2,2048]{2,1,0:T(2,128)(2,1)} reshape(bf16[32768,1,2,4]{3,2,1,0:T(2,128)(2,1)} %bitcast.208) | data formatting | bytes 1048576
  80.7 17.3 %all-to-all-start = ((bf16[64,2,2048]{2,1,0:T(2,128)(2,1)}), bf16[64,2,2048]{2,1,0:T(2,128)(2,1)S(1)}, u32[]{:S(2)}, u32[]{:S(2)}) async-start(bf16[64,2,2048]{2,1,0:T(2,128)(2,1)} %reshape.1203), calls=%async_computation | async-start | bytes 1048576 | tf_op jit(solution)/shard_map/all_to_all | solution.py:153
  98.0 1.1 bitcast_convert_fusion.1
  99.1 25.7 %copy.112 = bf16[1,2,4,32768]{2,1,0,3:T(2,128)(2,1)} copy(bf16[1,2,4,32768]{3,2,1,0:T(4,128)(2,1)S(1)} %copy-done.2) | data formatting | bytes 1048576 | tf_op args[0]
  125.7 31.8 %reshape.1207 = bf16[64,2,2048]{2,1,0:T(2,128)(2,1)} reshape(bf16[32768,1,2,4]{3,2,1,0:T(2,128)(2,1)} %bitcast.206) | data formatting | bytes 1048576
  157.9 37.0 %reshape.1204 = bf16[32768,1,2,4]{3,2,1,0:T(2,128)(2,1)} reshape(bf16[64,2,2048]{2,1,0:T(2,128)(2,1)S(1)} %all-to-all-done) | data formatting | bytes 1048576
  195.0 19.8 %reduce_sum.30 = bf16[4,2,512]{0,1,2:T(2,128)(2,1)S(1)} reduce(bf16[4,2,64,512]{0,1,3,2:T(2,128)(2,1)} %bitcast.207, bf16[]{:T(256)} %constant.203.clone.1), dimensions={2}, to_apply=%region_0.1 | reduce | flops 258048 | bytes 532482 | tf_op jit(solution)/shard_map/reduce_sum | solution.py:154
  214.9 0.7 broadcast_in_dim.7
  215.6 5.3 all-to-all-start.1
  220.9 4.8 all-to-all-done.1
  225.7 0.6 gather_fusion
  226.3 1.0 broadcast_in_dim.8
  227.3 12.7 %all-to-all-start.2 = ((bf16[64,4,2,512]{3,1,2,0:T(4,128)(2,1)}), bf16[64,4,2,512]{3,1,2,0:T(4,128)(2,1)S(1)}, u32[]{:S(2)}, u32[]{:S(2)}) async-start(bf16[64,4,2,512]{3,1,2,0:T(4,128)(2,1)} %broadcast_in_dim.8), calls=%async_computation.2 | async-start | bytes 1048576 | tf_op jit(solution)/shard_map/all_to_all | solution.py:23
  240.1 4.2 sine_multiply_fusion
  244.3 1.6 maximum_bitcast_fusion.11
  245.9 1.6 maximum_bitcast_fusion.9
  247.5 1.3 broadcast_multiply_fusion
  248.8 1.4 fusion.39
  250.2 6.2 all-to-all-done.2
  256.4 8.5 %all-to-all-start.4 = ((bf16[64,2,2048]{2,1,0:T(2,128)(2,1)}), bf16[64,2,2048]{2,1,0:T(2,128)(2,1)}, u32[]{:S(2)}, u32[]{:S(2)}) async-start(bf16[64,2,2048]{2,1,0:T(2,128)(2,1)} %reshape.1207), calls=%async_computation.4 | async-start | bytes 1048576 | tf_op jit(solution)/shard_map/all_to_all | solution.py:144
  265.5 0.7 slice_convert_fusion.1
  267.0 1.9 multiply_add_fusion
  268.9 3.6 add.526
  272.5 2.4 sub.117
  274.9 9.7 %fusion.13 = f32[16,2,32,8,128,1]{4,3,2,0,1,5:T(8,128)S(1)} fusion(f32[16,1,256,128]{3,2,1,0:T(8,128)} %sub.117, f32[16,1,256,128]{3,2,1,0:T(8,128)} %add.526, f32[1,2,256,256]{3,2,1,0:T(8,128)} %get-tuple-element.26, f32[1,2,256,256]{3,2,1,0:T(8,128)} %get-tuple-element.27), kind=kOutput, calls=%fused_computation.14 | convolution fusion | flops 6443761664 | bytes 9437184 | tf_op jit(solution)/shard_map/bcpq,dcsp->bdsq/dot_general | solution.py:93
  284.6 5.0 fusion.7
  289.6 4.7 fusion.10
  294.4 10.2 %fusion.14 = f32[16,2,256,128]{3,2,0,1:T(8,128)} fusion(f32[16,2,32,8,128]{4,2,0,1,3:T(8,128)S(1)} %fusion.10, f32[1,2,256,256]{3,2,1,0:T(8,128)S(1)} %copy-done.13, f32[1,2,256,256]{3,2,1,0:T(8,128)S(1)} %copy-done.12), kind=kOutput, calls=%fused_computation.15 | convolution fusion | flops 6442713088 | bytes 9437184 | tf_op jit(solution)/shard_map/bcpq,dcsp->bdsq/dot_general | solution.py:106
  304.6 5.7 reshape.1167
  310.2 4.2 subtract_reduce_fusion
  314.9 25.7 %copy.110 = bf16[1,2,4,32768]{2,1,0,3:T(2,128)(2,1)} copy(bf16[1,2,4,32768]{3,2,1,0:T(4,128)(2,1)S(1)} %fusion.33) | data formatting | bytes 1048576 | tf_op jit(solution)/shard_map/convert_element_type | solution.py:159
  340.6 31.8 %reshape.1205 = bf16[64,2,2048]{2,1,0:T(2,128)(2,1)} reshape(bf16[32768,1,2,4]{3,2,1,0:T(2,128)(2,1)} %bitcast.209) | data formatting | bytes 1048576
  372.5 12.3 %all-to-all-start.3 = ((bf16[64,2,2048]{2,1,0:T(2,128)(2,1)}), bf16[64,2,2048]{2,1,0:T(2,128)(2,1)S(1)}, u32[]{:S(2)}, u32[]{:S(2)}) async-start(bf16[64,2,2048]{2,1,0:T(2,128)(2,1)} %reshape.1205), calls=%async_computation.3 | async-start | bytes 1048576 | tf_op jit(solution)/shard_map/all_to_all | solution.py:160
  384.8 38.0 %reshape.1208 = bf16[32768,1,2,4]{3,2,1,0:T(2,128)(2,1)} reshape(bf16[64,2,2048]{2,1,0:T(2,128)(2,1)} %all-to-all-done.4) | data formatting | bytes 1048576
  422.8 32.8 %copy.113 = bf16[1,2,4,64,512]{4,2,3,1,0:T(4,128)(2,1)S(1)} copy(bf16[1,2,4,64,512]{2,1,4,3,0:T(2,128)(2,1)} %bitcast.210) | data formatting | bytes 1048576 | tf_op jit(solution)/shard_map/all_to_all | solution.py:144
  456.3 37.0 %reshape.1206 = bf16[32768,1,2,4]{3,2,1,0:T(2,128)(2,1)} reshape(bf16[64,2,2048]{2,1,0:T(2,128)(2,1)S(1)} %all-to-all-done.3) | data formatting | bytes 1048576
  493.4 32.8 %copy.111 = bf16[1,2,4,64,512]{4,2,3,1,0:T(4,128)(2,1)S(1)} copy(bf16[1,2,4,64,512]{2,1,4,3,0:T(2,128)(2,1)} %bitcast.211) | data formatting | bytes 1048576 | tf_op jit(solution)/shard_map/all_to_all | solution.py:160
  526.8 1.1 maximum_multiply_fusion.1
  528.5 156.6 %all-reduce.2.cloned.1.call-done = f32[4,256,256]{2,1,0:T(8,128)} async-done(((f32[4,256,256]{2,1,0:T(8,128)}), f32[4,256,256]{2,1,0:T(8,128)}) %all-reduce.2.cloned.1.call-update) | async-done | bytes 1048592 | tf_op jit(solution)/shard_map/psum | solution.py:178
  685.1 1.5 fusion.73
  686.6 1.4 fusion.74
  688.1 1.5 fusion.99
  691.0 21.6 %all_to_all.70 = bf16[1,2,256,512]{3,1,0,2:T(2,128)(2,1)S(1)} all-to-all(bf16[1,2,256,512]{3,1,0,2:T(2,128)(2,1)S(1)} %copy.115), channel_id=1, replica_groups=mesh['kpt'=8,'band'=64] {'band'}, dimensions={2} | all-to-all | bytes 1048576 | tf_op jit(solution)/shard_map/all_to_all | solution.py:188
  712.8 1.2 all_to_all.63
  (71 shorter events, 7.5 us)
Async XLA Ops:
  6.5 151.0 %copy-start = (s32[8,4]{0,1:T(4,128)S(1)}, s32[8,4]{0,1:T(4,128)}, u32[]{:S(2)}) copy-start(s32[8,4]{0,1:T(4,128)} %param.9) | copy-start | bytes 388
  48.8 49.2 %copy-start.2 = (bf16[1,2,4,32768]{3,2,1,0:T(4,128)(2,1)S(1)}, bf16[1,2,4,32768]{3,2,1,0:T(4,128)(2,1)}, u32[]{:S(2)}) copy-start(bf16[1,2,4,32768]{3,2,1,0:T(4,128)(2,1)} %param.5) | copy-start | bytes 1572868
  80.7 77.2 %all-to-all-start = ((bf16[64,2,2048]{2,1,0:T(2,128)(2,1)}), bf16[64,2,2048]{2,1,0:T(2,128)(2,1)S(1)}, u32[]{:S(2)}, u32[]{:S(2)}) async-start(bf16[64,2,2048]{2,1,0:T(2,128)(2,1)} %reshape.1203), calls=%async_computation | async-start | bytes 1048576 | tf_op jit(solution)/shard_map/all_to_all | solution.py:153
  99.1 25.7 %copy-start.15 = (f32[1,32768]{1,0:T(1,128)S(1)}, f32[1,32768]{1,0:T(1,128)}, u32[]{:S(2)}) copy-start(f32[1,32768]{1,0:T(1,128)} %param.7) | copy-start | bytes 393220
  215.6 10.1 %all-to-all-start.1 = ((bf16[8,1,4,2,512]{4,3,2,1,0:T(2,128)(2,1)}), bf16[8,1,4,2,512]{4,3,2,1,0:T(2,128)(2,1)S(1)}, u32[]{:S(2)}, u32[]{:S(2)}) async-start(bf16[8,1,4,2,512]{4,3,2,1,0:T(2,128)(2,1)} %broadcast_in_dim.7), calls=%async_computation.1 | async-start | bytes 131072 | tf_op jit(solution)/shard_map/all_to_all | solution.py:23
  227.3 29.1 %all-to-all-start.2 = ((bf16[64,4,2,512]{3,1,2,0:T(4,128)(2,1)}), bf16[64,4,2,512]{3,1,2,0:T(4,128)(2,1)S(1)}, u32[]{:S(2)}, u32[]{:S(2)}) async-start(bf16[64,4,2,512]{3,1,2,0:T(4,128)(2,1)} %broadcast_in_dim.8), calls=%async_computation.2 | async-start | bytes 1048576 | tf_op jit(solution)/shard_map/all_to_all | solution.py:23
  256.4 116.0 %all-to-all-start.4 = ((bf16[64,2,2048]{2,1,0:T(2,128)(2,1)}), bf16[64,2,2048]{2,1,0:T(2,128)(2,1)}, u32[]{:S(2)}, u32[]{:S(2)}) async-start(bf16[64,2,2048]{2,1,0:T(2,128)(2,1)} %reshape.1207), calls=%async_computation.4 | async-start | bytes 1048576 | tf_op jit(solution)/shard_map/all_to_all | solution.py:144
  265.5 1.5 copy-start.10
  265.5 1.5 copy-start.11
  266.9 2.0 copy-start.3
  274.9 9.7 %copy-start.5 = (f32[1,2,8,128,128]{4,3,1,0,2:T(8,128)S(1)}, f32[1,2,8,128,128]{4,3,1,0,2:T(8,128)}, u32[]{:S(2)}) copy-start(f32[1,2,8,128,128]{4,3,1,0,2:T(8,128)} %get-tuple-element.15) | copy-start | bytes 3145732
  274.9 9.7 %copy-start.6 = (f32[1,2,8,128,128]{4,3,1,0,2:T(8,128)S(1)}, f32[1,2,8,128,128]{4,3,1,0,2:T(8,128)}, u32[]{:S(2)}) copy-start(f32[1,2,8,128,128]{4,3,1,0,2:T(8,128)} %get-tuple-element.16) | copy-start | bytes 3145732
  284.6 5.0 copy-start.8
  284.6 5.0 copy-start.9
  289.6 4.7 copy-start.12
  289.6 4.7 copy-start.13
  304.6 5.7 copy-start.4
  310.2 4.2 copy-start.14
  372.5 83.8 %all-to-all-start.3 = ((bf16[64,2,2048]{2,1,0:T(2,128)(2,1)}), bf16[64,2,2048]{2,1,0:T(2,128)(2,1)S(1)}, u32[]{:S(2)}, u32[]{:S(2)}) async-start(bf16[64,2,2048]{2,1,0:T(2,128)(2,1)} %reshape.1205), calls=%async_computation.3 | async-start | bytes 1048576 | tf_op jit(solution)/shard_map/all_to_all | solution.py:160
  384.7 300.4 %all-reduce.2.cloned.1.call-start = ((), (), s32[]{:S(2)}) async-start(), calls=%async_computation.6 | async-start | bytes 2097152 | tf_op jit(solution)/shard_map/psum | solution.py:178
  685.1 4.4 copy-start.7
  690.4 23.5 %copy-start.1 = (s32[8,4]{0,1:T(4,128)S(1)}, s32[8,4]{0,1:T(4,128)}, u32[]{:S(2)}) copy-start(s32[8,4]{0,1:T(4,128)} %param.9) | copy-start | bytes 388
Sparse Core Ops, SparseCore 0:
  528.0 157.0 all-reduce.1
where the time goes:
time: 734 us; the launch traced here: 721 us
  local copies, waits for them, and re-layouts  373 us (51%)
  waiting for transfers between devices  168 us (23%)
  starting transfers between devices  56.1 us (8%)
  other arithmetic  41.9 us (6%)
  matrix products  35.7 us (5%)
  between operations  24.6 us (3%)
  blocking collectives  21.6 us (3%)
    unnamed x41, local copies, waits for them, and re-layouts  234 us
    psum x1, waiting for transfers between devices, body(): totals = lax.psum(partial_sums, 'band')  157 us
    all_to_all x1, local copies, waits for them, and re-layouts, body(): lax.all_to_all(orbitals, 'band', split_axis=3, concat_axis=2, tiled=True)  32.8 us
    all_to_all x1, local copies, waits for them, and re-layouts, body(): lax.all_to_all(values[None], 'band', split_axis=3, concat_axis=2, tiled=T...  32.8 us
    convert_element_type x1, local copies, waits for them, and re-layouts, body(): (potential * resident.astype(jnp.float32) + exchange).astype(jnp.bfloat16)  25.7 us
    broadcast_in_dim x1, local copies, waits for them, and re-layouts, body(): masked[None]  25.7 us
    all_to_all x1, blocking collectives, body(): lax.all_to_all(residual_slab, 'band', split_axis=2, concat_axis=3, tiled=...  21.6 us
    reduce_sum x1, other arithmetic, body(): shares = jnp.sum(arrived.astype(jnp.float32), axis=0).astype(jnp.bfloat16)  19.8 us
  transfers between devices with their start and end apart: 6, of which 3 were waited for; matrix products, arithmetic and copies ran while one was open for 35% of the time, Pallas kernels for 0%

commit v1 on v0

v1 whole, which is shorter than its diff:
```python
import functools

import jax
import jax.numpy as jnp
import numpy as np
from jax import lax
from jax.experimental import pallas as pl
from jax.experimental.pallas import tpu as pltpu
from jax.sharding import PartitionSpec as P

GRID = 32768
OWNERS = 4
SHARE = -0.25
SCALE = 1.6245
MESH = pl.DeviceIdType.MESH
F32 = jnp.float32
BF16 = jnp.bfloat16


def as_real(m):
    return np.block([[m.real, -m.imag], [m.imag, m.real]])


def tables():
    spot = np.arange(256)
    plane = (spot % 64) * 4 + spot // 64
    cell_x, cell_y = plane // 8, plane % 8
    freq_x, freq_y = spot % 32, spot // 32
    outer = np.exp(
        -2j * np.pi * (freq_x[:, None] * cell_x / 32 + freq_y[:, None] * cell_y / 8)
    )
    lane = np.arange(128)
    high, last = lane // 32, lane % 32
    inner = [
        np.exp(
            -2j
            * np.pi
            * ((h + 8 * high[:, None]) * high / 32 + last[:, None] * last / 32)
        )
        for h in range(8)
    ]
    first = (SCALE * as_real(outer)).astype(BF16)
    second = np.stack([(SCALE * as_real(m).T) for m in inner]).astype(BF16)
    return first, np.ascontiguousarray(first.T), second


def far_first(step):
    def offset(j):
        return 4 + ((j + 1) // 2) * (1 - 2 * (j % 2))

    return offset(step // 8), offset(step % 8)


def kernel(
    x, pot, kern, owners, partner, first_hbm, firstt_hbm, second_hbm,
    out,
    first, firstt, second, spread, bands, kgrid,
    osend, orecv, xs, sh, phsend, ph, msend, mrecv, mown, mall, mt,
    dens, mid, acc, vsend, vrecv, ys, psend, precv, cown, call, rsend,
    csem, ssem, rsem,
):
    me = lax.axis_index("band")
    mine = lax.axis_index("kpt")
    row, col = me // 8, me % 8

    def peer(step):
        dy, dz = far_first(step)
        return lax.rem(row + dy, 8) * 8 + lax.rem(col + dz, 8)

    barrier = pltpu.get_barrier_semaphore()

    def greet(step, _):
        pl.semaphore_signal(barrier, inc=1, device_id={"band": peer(step)}, device_id_type=MESH)
        return 0

    lax.fori_loop(0, 63, greet, 0)

    def greet_kpt(step, _):
        pl.semaphore_signal(
            barrier, inc=1, device_id={"kpt": lax.rem(mine + step, 8)}, device_id_type=MESH
        )
        return 0

    lax.fori_loop(1, 8, greet_kpt, 0)

    loads = [
        pltpu.make_async_copy(src, dst, csem.at[i])
        for i, (src, dst) in enumerate(
            ((first_hbm, first), (firstt_hbm, firstt), (second_hbm, second))
        )
    ]
    for load in loads:
        load.start()

    def spread_out(source, dst, which, f):
        for i in range(4):
            dst[which, i * 64 : (i + 1) * 64, :] = source[pl.ds(i * 512 + f, 64, stride=8), :]

    def pack(d, _):
        block = x[:, :, pl.ds(pl.multiple_of(d * 512, 512), 512)]
        wide = block.astype(F32).reshape(8, 512)
        for i in range(4):
            spread[pl.ds(pl.multiple_of(d * 8, 8) + i * 512, 8), :] = wide[:, i * 128 : (i + 1) * 128]
        osend[d] = wide.astype(BF16)
        return 0

    lax.fori_loop(0, 64, pack, 0)

    pl.semaphore_wait(barrier, 70)

    def to_all(n, source, dst):
        def go(step, _):
            p = peer(step)
            pltpu.make_async_remote_copy(
                src_ref=source(p),
                dst_ref=dst.at[me],
                send_sem=ssem.at[n],
                recv_sem=rsem.at[n],
                device_id={"band": p},
                device_id_type=MESH,
            ).start()
            return 0

        lax.fori_loop(0, 63, go, 0)

    def arrived(n, dst):
        part = dst.at[pl.ds(0, 63)]
        pltpu.make_async_copy(part, part, rsem.at[n]).wait()

    def left(n, dst):
        part = dst.at[pl.ds(0, 63)]
        pltpu.make_async_copy(part, part, ssem.at[n]).wait()

    orecv[me] = osend[me]
    to_all(0, lambda p: osend.at[p], orecv)

    for f in range(8):
        spread_out(spread, bands, f, f)
    lane128 = lax.broadcasted_iota(jnp.int32, (32, 128), 1)
    for h in range(8):
        tile = jnp.zeros((32, 128), F32)
        for j in range(4):
            piece = kern[pl.ds(2 * j + h // 4, 32, stride=8), :]
            shift = (j * 32 - (h % 4) * 32) % 128
            if shift:
                piece = pltpu.roll(piece, shift, 1)
            tile = jnp.where(lane128 // 32 == j, piece, tile)
        kgrid[h] = tile * (1.0 / (GRID * SCALE**4))

    arrived(0, orecv)
    xs[...] = orecv[...].astype(F32).reshape(512, 512).astype(BF16)

    line = lax.broadcasted_iota(jnp.int32, (8, 512), 0)
    place = lax.broadcasted_iota(jnp.int32, (8, 512), 1)
    want = jnp.zeros((8, 512), jnp.int32)
    for o in range(OWNERS):
        band = owners[o]
        base = (band // 4) * 8 + band % 4
        want = jnp.where(line // 2 == o, base + (line % 2) * 4, want)
    pick = jnp.where(place == want, 1.0, 0.0).astype(BF16)
    share = jnp.dot(pick, xs[...], preferred_element_type=F32).astype(BF16)
    sh[mine] = share

    def kpt_copy(step):
        return pltpu.make_async_remote_copy(
            src_ref=sh.at[mine],
            dst_ref=sh.at[mine],
            send_sem=ssem.at[8],
            recv_sem=rsem.at[8],
            device_id={"kpt": lax.rem(mine + step, 8)},
            device_id_type=MESH,
        )

    def kpt_go(step, _):
        kpt_copy(step).start()
        return 0

    lax.fori_loop(1, 8, kpt_go, 0)

    group = lax.broadcasted_iota(jnp.int32, (512, 512), 1) % 8 < 4

    def fold(gram):
        low = pltpu.roll(gram, 508, 0)
        swapped = jnp.where(group, pltpu.roll(low, 508, 1), -pltpu.roll(low, 4, 1))
        return ((gram + swapped) * (1.0 / GRID)).reshape(64, 8, 512)[:, :4, :]

    def widen(rows):
        flat = rows.reshape(256, 512)
        other = jnp.where(group[:256], -pltpu.roll(flat, 508, 1), pltpu.roll(flat, 4, 1))
        return jnp.concatenate([rows, other.reshape(64, 4, 512)], axis=1).reshape(512, 512)

    def gram_of(left_ref):
        return lax.dot_general(
            left_ref[...], xs[...], (((1,), (1,)), ((), ())), preferred_element_type=F32
        )

    msend[...] = fold(gram_of(xs)).astype(BF16)

    part7 = sh.at[pl.ds(0, 7)]
    pltpu.make_async_copy(part7, part7, rsem.at[8]).wait()
    wanted = jnp.zeros((8, 512), jnp.int32)
    for o in range(OWNERS):
        wanted = jnp.where(line // 2 == o, partner[mine, o], wanted)
    got = jnp.zeros((8, 512), F32)
    for k in range(8):
        got = jnp.where(wanted == k, sh[k].astype(F32), got)
    phsend[...] = got.astype(BF16)
    ph[me] = phsend[...]
    to_all(1, lambda p: phsend, ph)

    mrecv[me] = msend[me]
    to_all(2, lambda p: msend.at[p], mrecv)

    arrived(1, ph)
    for load in loads:
        load.wait()
    for i in range(4):
        at = slice(i * 128, (i + 1) * 128)
        spread[i * 512 : (i + 1) * 512, :] = ph[:, :, at].astype(F32).reshape(512, 128)

    def phase(f):
        return jnp.concatenate(
            [spread[pl.ds(i * 512 + f, 64, stride=8), :] for i in range(4)], axis=0
        )

    for o in range(OWNERS):
        ph_re, ph_im = phase(2 * o), phase(2 * o + 1)
        for b in range(4):
            b_re, b_im = bands[b], bands[4 + b]
            at = b * 128
            dens[0:256, at : at + 128] = (ph_re * b_re + ph_im * b_im).astype(BF16)
            dens[256:512, at : at + 128] = (ph_re * b_im - ph_im * b_re).astype(BF16)
        mid[:, o * 512 : (o + 1) * 512] = jnp.dot(
            first[...], dens[...], preferred_element_type=F32
        ).astype(BF16)

    arrived(2, mrecv)
    mown[...] = jnp.sum(mrecv[...].astype(F32), axis=0)
    mall[me] = mown[...]
    to_all(3, lambda p: mown, mall)

    def inner(h, _):
        r = pl.multiple_of(h * 32, 32)
        rows = jnp.concatenate(
            [
                jnp.concatenate(
                    [
                        mid[pl.ds(r + 256 * c, 32), f * 128 : (f + 1) * 128]
                        for c in range(2)
                    ],
                    axis=1,
                )
                for f in range(16)
            ],
            axis=0,
        )
        spectrum = jnp.dot(rows, second[h], preferred_element_type=F32)
        factor = jnp.concatenate([kgrid[h], kgrid[h]], axis=1)
        spectrum = (spectrum.reshape(16, 32, 256) * factor[None]).reshape(512, 256).astype(BF16)
        back = lax.dot_general(
            spectrum, second[h], (((1,), (1,)), ((), ())), preferred_element_type=F32
        ).astype(BF16)
        for f in range(16):
            for c in range(2):
                mid[pl.ds(r + 256 * c, 32), f * 128 : (f + 1) * 128] = back[
                    f * 32 : (f + 1) * 32, c * 128 : (c + 1) * 128
                ]
        return 0

    lax.fori_loop(0, 8, inner, 0)

    for o in range(OWNERS):
        ph_re, ph_im = phase(2 * o), phase(2 * o + 1)
        solved = jnp.dot(
            firstt[...], mid[:, o * 512 : (o + 1) * 512], preferred_element_type=F32
        )
        for b in range(4):
            s_re = solved[0:256, b * 128 : (b + 1) * 128]
            s_im = solved[256:512, b * 128 : (b + 1) * 128]
            t_re = ph_re * s_re - ph_im * s_im
            t_im = ph_re * s_im + ph_im * s_re
            if o:
                t_re = acc[b] + t_re
                t_im = acc[4 + b] + t_im
            acc[b] = t_re
            acc[4 + b] = t_im

    for i in range(4):
        local = pot[pl.ds(i, 64, stride=4), :]
        rows = slice(i * 64, (i + 1) * 64)
        for f in range(8):
            spread[pl.ds(i * 512 + f, 64, stride=8), :] = (
                local * bands[f, rows, :] + SHARE * acc[f, rows, :]
            )
    for i in range(4):
        part = spread[i * 512 : (i + 1) * 512, :].reshape(64, 8, 128)
        vsend[:, :, i * 128 : (i + 1) * 128] = part.astype(BF16)
    vrecv[me] = vsend[me]
    to_all(4, lambda p: vsend.at[p], vrecv)

    arrived(3, mall)
    mt[...] = widen(mall[...])

    arrived(4, vrecv)
    wide = vrecv[...].astype(F32).reshape(512, 512)
    ys[...] = wide.astype(BF16)
    psend[...] = fold(gram_of(ys)).astype(BF16)
    precv[me] = psend[me]
    to_all(5, lambda p: psend.at[p], precv)

    arrived(5, precv)
    proj = jnp.sum(precv[...].astype(F32), axis=0)
    coeff = 2.0 * proj - jnp.dot(
        proj, mt[...], precision=lax.Precision.HIGHEST, preferred_element_type=F32
    )
    cown[...] = coeff.astype(BF16)
    call[me] = cown[...]
    to_all(6, lambda p: cown, call)

    arrived(6, call)
    mixing = widen(call[...].astype(F32)).astype(BF16)
    correction = jnp.dot(mixing, xs[...], preferred_element_type=F32)
    rsend[...] = (ys[...].astype(F32) - correction).reshape(64, 8, 512).astype(BF16)
    out[me] = rsend[me]
    to_all(7, lambda p: rsend.at[p], out)
    arrived(7, out)

    left(0, osend)
    left(1, ph)
    left(2, msend)
    left(3, mall)
    left(4, vsend)
    left(5, psend)
    left(6, call)
    left(7, rsend)
    pltpu.make_async_copy(part7, part7, ssem.at[8]).wait()


def unpack(block, out):
    def one(d, _):
        wide = block[d].astype(F32)
        at = pl.ds(pl.multiple_of(d * 512, 512), 512)
        out[:, :, at] = wide.reshape(2, 4, 512).astype(BF16)
        return 0

    lax.fori_loop(0, 64, one, 0)


def body(orbitals, potential, kernel_grid, owners, partner):
    first, firstt, second = tables()
    vmem = pl.BlockSpec(memory_space=pltpu.VMEM)
    smem = pl.BlockSpec(memory_space=pltpu.SMEM)
    anywhere = pl.BlockSpec(memory_space=pl.ANY)
    slab = (64, 8, 512)
    thin = (64, 4, 512)
    block = pl.pallas_call(
        kernel,
        out_shape=jax.ShapeDtypeStruct(slab, BF16),
        in_specs=[vmem, vmem, vmem, smem, smem, anywhere, anywhere, anywhere],
        out_specs=vmem,
        scratch_shapes=[
            pltpu.VMEM((512, 512), BF16),
            pltpu.VMEM((512, 512), BF16),
            pltpu.VMEM((8, 256, 256), BF16),
            pltpu.VMEM((2048, 128), F32),
            pltpu.VMEM((8, 256, 128), F32),
            pltpu.VMEM((8, 32, 128), F32),
            pltpu.VMEM(slab, BF16),
            pltpu.VMEM(slab, BF16),
            pltpu.VMEM((512, 512), BF16),
            pltpu.VMEM((8, 8, 512), BF16),
            pltpu.VMEM((8, 512), BF16),
            pltpu.VMEM(slab, BF16),
            pltpu.VMEM(thin, BF16),
            pltpu.VMEM(thin, BF16),
            pltpu.VMEM((4, 512), F32),
            pltpu.VMEM(thin, F32),
            pltpu.VMEM((512, 512), F32),
            pltpu.VMEM((512, 512), BF16),
            pltpu.VMEM((512, 2048), BF16),
            pltpu.VMEM((8, 256, 128), F32),
            pltpu.VMEM(slab, BF16),
            pltpu.VMEM(slab, BF16),
            pltpu.VMEM((512, 512), BF16),
            pltpu.VMEM(thin, BF16),
            pltpu.VMEM(thin, BF16),
            pltpu.VMEM((4, 512), BF16),
            pltpu.VMEM(thin, BF16),
            pltpu.VMEM(slab, BF16),
            pltpu.SemaphoreType.DMA((3,)),
            pltpu.SemaphoreType.DMA((9,)),
            pltpu.SemaphoreType.DMA((9,)),
        ],
        compiler_params=pltpu.CompilerParams(
            collective_id=0, has_side_effects=True, vmem_limit_bytes=60 << 20
        ),
        name="exchange_residual",
    )(
        orbitals[0],
        potential.reshape(256, 128),
        kernel_grid.reshape(256, 128),
        owners,
        partner,
        first,
        firstt,
        second,
    )
    out = pl.pallas_call(
        unpack,
        out_shape=jax.ShapeDtypeStruct((2, 4, GRID), BF16),
        in_specs=[vmem],
        out_specs=vmem,
        name="unpack",
    )(block)
    return out[None]


def solution(mesh):
    in_specs = (P("kpt", None, "band", None), P(), P("kpt", None), P(), P())
    out_specs = P("kpt", None, "band", None)
    return jax.shard_map(body, mesh=mesh, in_specs=in_specs, out_specs=out_specs, check_vma=False)
```

time: 734 us -> 129 us (0.18); the launches traced: 721 us -> 129 us
  local copies, waits for them, and re-layouts: 373 us -> 1.35 us
  waiting for transfers between devices: 168 us -> 0 us
  Pallas kernels: 0 us -> 128 us
  starting transfers between devices: 56.1 us -> 0 us
  other arithmetic: 41.9 us -> 0 us
  matrix products: 35.7 us -> 0 us
  between operations: 24.6 us -> 0.01 us
  blocking collectives: 21.6 us -> 0 us
    unnamed x41 -> x3, local copies, waits for them, and re-layouts: 234 us -> 1.35 us
    psum x1 -> x0, waiting for transfers between devices: 157 us -> none  [body(): totals = lax.psum(partial_sums, 'band')]
    pallas_call x0 -> x2, Pallas kernels: none -> 128 us  [the longest x1 125 us: body(): pl.pallas_call(kernel, out_shape=jax.ShapeDtypeStruct(slab, BF16), in_spe...]
    all_to_all x4 -> x0, local copies, waits for them, and re-layouts: 66.9 us -> none  [the longest x1 32.8 us: body(): lax.all_to_all(orbitals, 'band', split_axis=3, concat_axis=2, tiled=True)]
    all_to_all x5 -> x0, starting transfers between devices: 56 us -> none  [the longest x2 18 us: copy_for_each(): lax.all_to_all(jnp.broadcast_to(array[None], (peers, *array.shape)), axis...]
    dot_general x11 -> x0, matrix products: 35.7 us -> none  [the longest x1 10.2 us: exchange_field(): jnp.einsum('bcpq,dcsp->bdsq', current, rotation(plain_angles, -1.0), prec...]
    broadcast_in_dim x3 -> x0, local copies, waits for them, and re-layouts: 27.4 us -> none  [the longest x1 25.7 us: body(): masked[None]]
    convert_element_type x3 -> x0, local copies, waits for them, and re-layouts: 26.6 us -> none  [the longest x1 25.7 us: body(): (potential * resident.astype(jnp.float32) + exchange).astype(jnp.bfloat16)]
  transfers between devices with their start and end apart: 6 -> 0, of which waited for: 3 -> 0; matrix products, arithmetic and copies ran while one was open for 35% -> 0% of each run, Pallas kernels for 0% -> 0%
where the time goes in v1:
time: 129 us
  Pallas kernels  128 us (99%)
  local copies, waits for them, and re-layouts  1.35 us (1%)
    pallas_call x1, Pallas kernels, body(): pl.pallas_call(kernel, out_shape=jax.ShapeDtypeStruct(slab, BF16), in_spe...  125 us

profile of v1, /device:TPU:1, one launch (start us, length us, event | category | flops | bytes accessed | tf_op | source)
XLA Modules:
  0.0 129.1 jit_solution(10300896206878671629)
XLA Ops:
  0.0 0.0 copy-start
  0.0 0.7 copy-done
  0.7 0.7 copy.9.partner
  1.4 125.3 %exchange_residual.1.block = bf16[64,8,512]{2,1,0:T(8,128)(2,1)} custom-call(bf16[2,4,32768]{2,1,0:T(4,128)(2,1)} %bitcast.4, f32[256,128]{1,0:T(8,128)} %bitcast.5, f32[256,128]{1,0:T(8,128)} %bitcast.6, s32[4]{0:T(128)} %owners.1, s32[8,4]{1,0:T(8,128)} %copy.9.partner, bf16[512,512]{1,0:T(8,128)(2,1)} %constant.6.clone.first_hbm, ...), custom_call_target="tpu_custom_call" | custom-call | tf_op jit(solution)/shard_map/exchange_residual/pallas_call | solution.py:356
  126.7 2.4 %unpack.1 = bf16[2,4,32768]{2,1,0:T(4,128)(2,1)} custom-call(bf16[64,8,512]{2,1,0:T(8,128)(2,1)} %exchange_residual.1.block), custom_call_target="tpu_custom_call" | custom-call | tf_op jit(solution)/shard_map/unpack/pallas_call | solution.py:408
Async XLA Ops:
  0.0 0.7 copy-start

commit v2 on v1

v2 whole, which is shorter than its diff:
```python
import jax
import jax.numpy as jnp
import numpy as np
from jax import lax
from jax.experimental import pallas as pl
from jax.experimental.pallas import tpu as pltpu
from jax.sharding import PartitionSpec as P

GRID = 32768
OWNERS = 4
SHARE = -0.25
SCALE = 1.6245
MESH = pl.DeviceIdType.MESH
F32 = jnp.float32
BF16 = jnp.bfloat16


def as_real(m):
    return np.block([[m.real, -m.imag], [m.imag, m.real]])


def tables():
    spot = np.arange(256)
    plane = (spot % 64) * 4 + spot // 64
    cell_x, cell_y = plane // 8, plane % 8
    freq_x, freq_y = spot % 32, spot // 32
    outer = np.exp(
        -2j * np.pi * (freq_x[:, None] * cell_x / 32 + freq_y[:, None] * cell_y / 8)
    )
    lane = np.arange(128)
    high, last = lane // 32, lane % 32
    inner = [
        np.exp(
            -2j
            * np.pi
            * ((h + 8 * high[:, None]) * high / 32 + last[:, None] * last / 32)
        )
        for h in range(8)
    ]
    first = (SCALE * as_real(outer)).astype(BF16)
    second = np.stack([(SCALE * as_real(m).T) for m in inner]).astype(BF16)
    return first, np.ascontiguousarray(first.T), second


def offset(j):
    return 4 + ((j + 1) // 2) * (1 - 2 * (j % 2))


def kernel(
    x_hbm, pot_hbm, kern_hbm, owners, partner, first_hbm, firstt_hbm, second_hbm,
    out,
    x, pot, kern, first, firstt, second, spread, bands, kgrid,
    osend, orecv, xs, sh, ph_a, ph_b, msend, mrecv, mown, mall, mt,
    dens, mid, acc, vsend, vrecv, ys, psend, precv, cown, call, rsend, rrecv, result,
    csem, ssem, rsem, gsem, fsem,
):
    me = lax.axis_index("band")
    mine = lax.axis_index("kpt")
    row, col = me // 8, me % 8

    loads = [
        pltpu.make_async_copy(src, dst, csem.at[i])
        for i, (src, dst) in enumerate(
            (
                (x_hbm, x),
                (pot_hbm, pot),
                (kern_hbm, kern),
                (first_hbm, first),
                (firstt_hbm, firstt),
                (second_hbm, second),
            )
        )
    ]
    for load in loads:
        load.start()

    def around(place, j):
        return lax.rem(place + offset(j), 8)

    barrier = pltpu.get_barrier_semaphore()

    def greet(step, _):
        peer = around(row, step // 8) * 8 + around(col, step % 8)
        pl.semaphore_signal(barrier, inc=1, device_id={"band": peer}, device_id_type=MESH)
        return 0

    lax.fori_loop(0, 63, greet, 0)

    def greet_kpt(step, _):
        pl.semaphore_signal(
            barrier, inc=1, device_id={"kpt": lax.rem(mine + step, 8)}, device_id_type=MESH
        )
        return 0

    lax.fori_loop(1, 8, greet_kpt, 0)

    loads[0].wait()

    def pack(d, _):
        block = x[:, :, pl.ds(pl.multiple_of(d * 512, 512), 512)]
        wide = block.astype(F32).reshape(8, 512)
        for i in range(4):
            spread[pl.ds(pl.multiple_of(d * 8, 8) + i * 512, 8), :] = wide[
                :, i * 128 : (i + 1) * 128
            ]
        osend[d] = wide.astype(BF16)
        return 0

    lax.fori_loop(0, 64, pack, 0)
    pl.semaphore_wait(barrier, 70)

    def send(source, target, peer, n, arrival):
        pltpu.make_async_remote_copy(
            src_ref=source,
            dst_ref=target,
            send_sem=ssem.at[n],
            recv_sem=arrival,
            device_id={"band": peer},
            device_id_type=MESH,
        ).start()

    def wait(sem, dst, count):
        part = dst.at[pl.ds(0, count)]
        pltpu.make_async_copy(part, part, sem).wait()

    def to_all(n, source, dst, arrival):
        def go(step, _):
            peer = around(row, step // 8) * 8 + around(col, step % 8)
            send(source(peer), dst.at[me], peer, n, arrival(step // 8))
            return 0

        lax.fori_loop(0, 63, go, 0)

    def to_row(n, base, count, source, dst, arrival):
        def go(j, _):
            peer = base + around(col, j)
            send(source(peer), dst.at[me], peer, n, arrival)
            return 0

        lax.fori_loop(0, count, go, 0)

    def by_rows(step):
        def run(g, _):
            step(g, 8)
            return 0

        lax.fori_loop(0, 7, run, 0)
        step(7, 7)

    orecv[me] = osend[me]
    to_all(0, lambda p: osend.at[p], orecv, lambda g: rsem.at[0])

    for f in range(8):
        for i in range(4):
            bands[f, i * 64 : (i + 1) * 64, :] = spread[pl.ds(i * 512 + f, 64, stride=8), :]
    loads[2].wait()
    lane128 = lax.broadcasted_iota(jnp.int32, (32, 128), 1)
    for h in range(8):
        tile = jnp.zeros((32, 128), F32)
        for j in range(4):
            piece = kern[pl.ds(2 * j + h // 4, 32, stride=8), :]
            shift = (j * 32 - (h % 4) * 32) % 128
            if shift:
                piece = pltpu.roll(piece, shift, 1)
            tile = jnp.where(lane128 // 32 == j, piece, tile)
        kgrid[h] = tile * (1.0 / (GRID * SCALE**4))

    wait(rsem.at[0], orecv, 63)
    xs[...] = orecv[...].astype(F32).reshape(512, 512).astype(BF16)

    line = lax.broadcasted_iota(jnp.int32, (8, 512), 0)
    place = lax.broadcasted_iota(jnp.int32, (8, 512), 1)
    want = jnp.zeros((8, 512), jnp.int32)
    for o in range(OWNERS):
        band = owners[o]
        base = (band // 4) * 8 + band % 4
        want = jnp.where(line // 2 == o, base + (line % 2) * 4, want)
    pick = jnp.where(place == want, 1.0, 0.0).astype(BF16)
    share = jnp.dot(pick, xs[...], preferred_element_type=F32).astype(BF16)
    sh[mine] = share

    def kpt_go(step, _):
        pltpu.make_async_remote_copy(
            src_ref=sh.at[mine],
            dst_ref=sh.at[mine],
            send_sem=ssem.at[1],
            recv_sem=rsem.at[1],
            device_id={"kpt": lax.rem(mine + step, 8)},
            device_id_type=MESH,
        ).start()
        return 0

    lax.fori_loop(1, 8, kpt_go, 0)

    def fold(gram):
        rows = gram.shape[0]
        half = lax.broadcasted_iota(jnp.int32, gram.shape, 1) % 8 < 4
        low = pltpu.roll(gram, rows - 4, 0)
        swapped = jnp.where(half, pltpu.roll(low, 508, 1), -pltpu.roll(low, 4, 1))
        sums = ((gram + swapped) * (1.0 / GRID)).reshape(rows // 8, 8, 512)[:, :4, :]
        return sums.reshape(rows // 2, 512)

    def widen(flat):
        half = lax.broadcasted_iota(jnp.int32, flat.shape, 1) % 8 < 4
        other = jnp.where(half, -pltpu.roll(flat, 508, 1), pltpu.roll(flat, 4, 1))
        count = flat.shape[0] // 4
        both = [flat.reshape(count, 4, 512), other.reshape(count, 4, 512)]
        return jnp.concatenate(both, axis=1).reshape(count * 8, 512)

    def ahead(shape, base):
        line = lax.broadcasted_iota(jnp.int32, shape, 0)
        lane = lax.broadcasted_iota(jnp.int32, shape, 1)
        return lane - (base + line // 4) * 8 - line % 4

    def halve(flat, base):
        high = flat.astype(BF16).astype(F32)
        rest = pltpu.roll(flat - high, 4, 1)
        return jnp.where(ahead(flat.shape, base) == 4, rest, high).astype(BF16)

    def join(flat, base):
        at = ahead(flat.shape, base)
        whole = flat + pltpu.roll(flat, 508, 1)
        return jnp.where(at == 0, whole, jnp.where(at == 4, 0.0, flat))

    def gram_of(rows):
        return lax.dot_general(
            rows, xs[...], (((1,), (1,)), ((), ())), preferred_element_type=F32
        )

    msend[...] = halve(fold(gram_of(xs[...])), 0).reshape(64, 4, 512)

    wait(rsem.at[1], sh, 7)
    wanted = jnp.zeros((8, 512), jnp.int32)
    for o in range(OWNERS):
        wanted = jnp.where(line // 2 == o, partner[o, mine], wanted)
    got = jnp.zeros((8, 512), F32)
    for k in range(8):
        got = jnp.where(wanted == k, sh[k].astype(F32), got)

    turned = col * 8 + row
    ph_a[me] = got[:, :256].astype(BF16)
    ph_b[turned] = got[:, 256:].astype(BF16)

    def spread_one(j, _):
        send(ph_a.at[me], ph_a.at[me], row * 8 + around(col, j), 2, rsem.at[2])
        send(ph_b.at[turned], ph_b.at[turned], around(row, j) * 8 + col, 10, rsem.at[3])
        return 0

    lax.fori_loop(0, 7, spread_one, 0)
    wait(rsem.at[2], ph_a, 7)
    wait(rsem.at[3], ph_b, 7)

    def spread_all(j, _):
        part_a = ph_a.at[pl.ds(row * 8, 8)]
        part_b = ph_b.at[pl.ds(col * 8, 8)]
        send(part_a, part_a, around(row, j) * 8 + col, 3, rsem.at[4])
        send(part_b, part_b, row * 8 + around(col, j), 11, rsem.at[5])
        return 0

    lax.fori_loop(0, 7, spread_all, 0)

    mrecv[me] = msend[me]
    to_all(4, lambda p: msend.at[p], mrecv, lambda g: rsem.at[6])

    wait(rsem.at[4], ph_a, 56)
    wait(rsem.at[5], ph_b, 56)
    for i in range(4):
        source = ph_a if i < 2 else ph_b
        at = slice((i % 2) * 128, (i % 2 + 1) * 128)
        spread[i * 512 : (i + 1) * 512, :] = source[:, :, at].astype(F32).reshape(512, 128)

    def phase(f):
        parts = [spread[pl.ds(i * 512 + f, 64, stride=8), :] for i in range(2)]
        for i in range(2, 4):
            for r in range(8):
                parts.append(spread[pl.ds(i * 512 + r * 8 + f, 8, stride=64), :])
        return jnp.concatenate(parts, axis=0)

    for load in loads[3:]:
        load.wait()
    for o in range(OWNERS):
        ph_re, ph_im = phase(2 * o), phase(2 * o + 1)
        for b in range(4):
            b_re, b_im = bands[b], bands[4 + b]
            at = b * 128
            dens[0:256, at : at + 128] = (ph_re * b_re + ph_im * b_im).astype(BF16)
            dens[256:512, at : at + 128] = (ph_re * b_im - ph_im * b_re).astype(BF16)
        mid[:, o * 512 : (o + 1) * 512] = jnp.dot(
            first[...], dens[...], preferred_element_type=F32
        ).astype(BF16)

    def inner(h, _):
        r = pl.multiple_of(h * 32, 32)
        rows = jnp.concatenate(
            [
                jnp.concatenate(
                    [
                        mid[pl.ds(r + 256 * c, 32), f * 128 : (f + 1) * 128]
                        for c in range(2)
                    ],
                    axis=1,
                )
                for f in range(16)
            ],
            axis=0,
        )
        spectrum = jnp.dot(rows, second[h], preferred_element_type=F32)
        factor = jnp.concatenate([kgrid[h], kgrid[h]], axis=1)
        spectrum = (spectrum.reshape(16, 32, 256) * factor[None]).reshape(512, 256).astype(BF16)
        back = lax.dot_general(
            spectrum, second[h], (((1,), (1,)), ((), ())), preferred_element_type=F32
        ).astype(BF16)
        for f in range(16):
            for c in range(2):
                mid[pl.ds(r + 256 * c, 32), f * 128 : (f + 1) * 128] = back[
                    f * 32 : (f + 1) * 32, c * 128 : (c + 1) * 128
                ]
        return 0

    lax.fori_loop(0, 8, inner, 0)

    wait(rsem.at[6], mrecv, 63)
    margin = join(jnp.sum(mrecv[...].astype(F32), axis=0), me)
    mown[...] = halve(margin, me)
    mall[me] = mown[...]
    to_all(5, lambda p: mown, mall, lambda g: rsem.at[7])

    for o in range(OWNERS):
        ph_re, ph_im = phase(2 * o), phase(2 * o + 1)
        solved = jnp.dot(
            firstt[...], mid[:, o * 512 : (o + 1) * 512], preferred_element_type=F32
        )
        for b in range(4):
            s_re = solved[0:256, b * 128 : (b + 1) * 128]
            s_im = solved[256:512, b * 128 : (b + 1) * 128]
            t_re = ph_re * s_re - ph_im * s_im
            t_im = ph_re * s_im + ph_im * s_re
            if o:
                t_re = acc[b] + t_re
                t_im = acc[4 + b] + t_im
            acc[b] = t_re
            acc[4 + b] = t_im

    loads[1].wait()
    for i in range(4):
        local = pot[pl.ds(i, 64, stride=4), :]
        rows = slice(i * 64, (i + 1) * 64)
        for f in range(8):
            spread[pl.ds(i * 512 + f, 64, stride=8), :] = (
                local * bands[f, rows, :] + SHARE * acc[f, rows, :]
            )
    for i in range(4):
        part = spread[i * 512 : (i + 1) * 512, :].reshape(64, 8, 128)
        vsend[:, :, i * 128 : (i + 1) * 128] = part.astype(BF16)
    vrecv[me] = vsend[me]
    to_all(6, lambda p: vsend.at[p], vrecv, lambda g: gsem.at[0, g])

    wait(rsem.at[7], mall, 63)
    mt[...] = widen(join(mall[...].astype(F32).reshape(256, 512), 0))

    def take_values(g, count):
        source = lax.rem(row - offset(g) + 8, 8)
        base = pl.multiple_of(source * 8, 8)
        wait(gsem.at[0, g], vrecv, count)
        rows = vrecv[pl.ds(base, 8)].astype(F32).reshape(64, 512).astype(BF16)
        ys[pl.ds(pl.multiple_of(source * 64, 64), 64), :] = rows
        psend[pl.ds(base, 8)] = halve(fold(gram_of(rows)), base).reshape(8, 4, 512)
        to_row(7, base, count, lambda p: psend.at[p], precv, rsem.at[8])

    by_rows(take_values)
    precv[me] = psend[me]
    wait(rsem.at[8], precv, 63)
    proj = join(jnp.sum(precv[...].astype(F32), axis=0), me)
    coeff = 2.0 * proj - jnp.dot(
        proj, mt[...], precision=lax.Precision.HIGHEST, preferred_element_type=F32
    )
    cown[...] = coeff.astype(BF16)
    call[me] = cown[...]
    to_all(8, lambda p: cown, call, lambda g: gsem.at[1, g])

    def take_coefficients(g, count):
        source = lax.rem(row - offset(g) + 8, 8)
        base = pl.multiple_of(source * 8, 8)
        wait(gsem.at[1, g], call, count)
        mixing = widen(call[pl.ds(base, 8)].astype(F32).reshape(32, 512)).astype(BF16)
        correction = jnp.dot(mixing, xs[...], preferred_element_type=F32)
        own = ys[pl.ds(pl.multiple_of(source * 64, 64), 64), :].astype(F32)
        rsend[pl.ds(base, 8)] = (own - correction).reshape(8, 8, 512).astype(BF16)
        to_row(9, base, count, lambda p: rsend.at[p], rrecv, gsem.at[2, g])

    by_rows(take_coefficients)
    rrecv[me] = rsend[me]

    def take_residuals(g, count):
        source = around(row, g)
        wait(gsem.at[2, g], rrecv, count)
        base = pl.multiple_of(source * 4096, 4096)
        for s in range(8):
            wide = rrecv[source * 8 + s].astype(F32).reshape(2, 4, 512)
            result[:, :, pl.ds(base + s * 512, 512)] = wide.astype(BF16)
        cells = pl.ds(base, 4096)
        pltpu.make_async_copy(result.at[:, :, cells], out.at[:, :, cells], fsem).start()

    by_rows(take_residuals)
    pltpu.make_async_copy(result, out, fsem).wait()

    for n, ref in (
        (0, osend), (4, msend), (5, mall), (6, vsend), (7, psend), (8, call), (9, rsend)
    ):
        wait(ssem.at[n], ref, 63)
    wait(ssem.at[1], sh, 7)
    for n, ref in ((2, ph_a), (10, ph_b)):
        wait(ssem.at[n], ref, 7)
    for n, ref in ((3, ph_a), (11, ph_b)):
        wait(ssem.at[n], ref, 56)


def body(orbitals, potential, kernel_grid, owners, partner):
    first, firstt, second = tables()
    smem = pl.BlockSpec(memory_space=pltpu.SMEM)
    anywhere = pl.BlockSpec(memory_space=pl.ANY)
    slab = (64, 8, 512)
    thin = (64, 4, 512)
    out = pl.pallas_call(
        kernel,
        out_shape=jax.ShapeDtypeStruct((2, 4, GRID), BF16),
        in_specs=[anywhere, anywhere, anywhere, smem, smem, anywhere, anywhere, anywhere],
        out_specs=anywhere,
        scratch_shapes=[
            pltpu.VMEM((2, 4, GRID), BF16),
            pltpu.VMEM((256, 128), F32),
            pltpu.VMEM((256, 128), F32),
            pltpu.VMEM((512, 512), BF16),
            pltpu.VMEM((512, 512), BF16),
            pltpu.VMEM((8, 256, 256), BF16),
            pltpu.VMEM((2048, 128), F32),
            pltpu.VMEM((8, 256, 128), F32),
            pltpu.VMEM((8, 32, 128), F32),
            pltpu.VMEM(slab, BF16),
            pltpu.VMEM(slab, BF16),
            pltpu.VMEM((512, 512), BF16),
            pltpu.VMEM((8, 8, 512), BF16),
            pltpu.VMEM((64, 8, 256), BF16),
            pltpu.VMEM((64, 8, 256), BF16),
            pltpu.VMEM(thin, BF16),
            pltpu.VMEM(thin, BF16),
            pltpu.VMEM((4, 512), BF16),
            pltpu.VMEM(thin, BF16),
            pltpu.VMEM((512, 512), F32),
            pltpu.VMEM((512, 512), BF16),
            pltpu.VMEM((512, 2048), BF16),
            pltpu.VMEM((8, 256, 128), F32),
            pltpu.VMEM(slab, BF16),
            pltpu.VMEM(slab, BF16),
            pltpu.VMEM((512, 512), BF16),
            pltpu.VMEM(thin, BF16),
            pltpu.VMEM(thin, BF16),
            pltpu.VMEM((4, 512), BF16),
            pltpu.VMEM(thin, BF16),
            pltpu.VMEM(slab, BF16),
            pltpu.VMEM(slab, BF16),
            pltpu.VMEM((2, 4, GRID), BF16),
            pltpu.SemaphoreType.DMA((6,)),
            pltpu.SemaphoreType.DMA((12,)),
            pltpu.SemaphoreType.DMA((9,)),
            pltpu.SemaphoreType.DMA((3, 8)),
            pltpu.SemaphoreType.DMA,
        ],
        compiler_params=pltpu.CompilerParams(
            collective_id=0, has_side_effects=True, vmem_limit_bytes=60 << 20
        ),
        name="exchange_residual",
    )(
        orbitals[0],
        potential.reshape(256, 128),
        kernel_grid.reshape(256, 128),
        owners,
        partner.T,
        first,
        firstt,
        second,
    )
    return out[None]


def solution(mesh):
    in_specs = (P("kpt", None, "band", None), P(), P("kpt", None), P(), P())
    out_specs = P("kpt", None, "band", None)
    return jax.shard_map(body, mesh=mesh, in_specs=in_specs, out_specs=out_specs, check_vma=False)
```

time: 129 us -> 111 us (0.86)
  Pallas kernels: 128 us -> 109 us
    pallas_call x2 -> x1, Pallas kernels: 128 us -> 109 us  [body(): pl.pallas_call(kernel, out_shape=jax.ShapeDtypeStruct((2, 4, GRID), BF16)...]
where the time goes in v2:
time: 111 us
  Pallas kernels  109 us (98%)
  local copies, waits for them, and re-layouts  2.02 us (2%)
    pallas_call x1, Pallas kernels, body(): pl.pallas_call(kernel, out_shape=jax.ShapeDtypeStruct((2, 4, GRID), BF16)...  109 us

profile of v2, /device:TPU:1, one launch (start us, length us, event | category | flops | bytes accessed | tf_op | source)
XLA Modules:
  0.0 110.6 jit_solution(171186513764364537)
XLA Ops:
  0.0 108.6 %exchange_residual.1 = bf16[2,4,32768]{2,1,0:T(4,128)(2,1)} custom-call(bf16[2,4,32768]{2,1,0:T(4,128)(2,1)} %bitcast.6, f32[256,128]{1,0:T(8,128)} %bitcast.7, f32[256,128]{1,0:T(8,128)} %bitcast.8, s32[4]{0:T(128)} %owners.1, s32[4,8]{1,0:T(4,128)} %bitcast.9, bf16[512,512]{1,0:T(8,128)(2,1)} %constant.6.clone.first_hbm, ...), custom_call_target="tpu_custom_call" | custom-call | tf_op jit(solution)/shard_map/exchange_residual/pallas_call | solution.py:424
  108.6 2.0 %copy.10 = bf16[1,2,4,32768]{3,2,1,0:T(4,128)(2,1)} copy(bf16[1,2,4,32768]{3,2,1,0:T(4,128)(2,1)} %bitcast.5) | data formatting | bytes 1048576

commit v3 on v2

--- a/solution.py
+++ b/solution.py
@@ -50,9 +50,9 @@
     x_hbm, pot_hbm, kern_hbm, owners, partner, first_hbm, firstt_hbm, second_hbm,
     out,
     x, pot, kern, first, firstt, second, spread, bands, kgrid,
-    osend, orecv, xs, sh, ph_a, ph_b, msend, mrecv, mown, mall, mt,
+    osend, orecv, xs, sh, ph_a, ph_b, msend, mrecv, m_a, m_b, mall, mt,
     dens, mid, acc, vsend, vrecv, ys, psend, precv, cown, call, rsend, rrecv, result,
-    csem, ssem, rsem, gsem, fsem,
+    csem, ssem, rsem, gsem, fsem, asem,
 ):
     me = lax.axis_index("band")
     mine = lax.axis_index("kpt")
@@ -147,6 +147,14 @@
         lax.fori_loop(0, 7, run, 0)
         step(7, 7)
 
+    def by_near_rows(step):
+        def run(i, _):
+            step(6 - i, 8)
+            return 0
+
+        step(7, 7)
+        lax.fori_loop(0, 7, run, 0)
+
     orecv[me] = osend[me]
     to_all(0, lambda p: osend.at[p], orecv, lambda g: rsem.at[0])
 
@@ -242,22 +250,32 @@
     ph_b[turned] = got[:, 256:].astype(BF16)
 
     def spread_one(j, _):
-        send(ph_a.at[me], ph_a.at[me], row * 8 + around(col, j), 2, rsem.at[2])
-        send(ph_b.at[turned], ph_b.at[turned], around(row, j) * 8 + col, 10, rsem.at[3])
+        send(ph_a.at[me], ph_a.at[me], row * 8 + around(col, j), 2, asem.at[0, j])
+        send(ph_b.at[turned], ph_b.at[turned], around(row, j) * 8 + col, 10, asem.at[1, j])
         return 0
 
     lax.fori_loop(0, 7, spread_one, 0)
-    wait(rsem.at[2], ph_a, 7)
-    wait(rsem.at[3], ph_b, 7)
-
-    def spread_all(j, _):
-        part_a = ph_a.at[pl.ds(row * 8, 8)]
-        part_b = ph_b.at[pl.ds(col * 8, 8)]
-        send(part_a, part_a, around(row, j) * 8 + col, 3, rsem.at[4])
-        send(part_b, part_b, row * 8 + around(col, j), 11, rsem.at[5])
-        return 0
-
-    lax.fori_loop(0, 7, spread_all, 0)
+
+    def pass_on(slot_a, slot_b):
+        def go(j, _):
+            send(ph_a.at[slot_a], ph_a.at[slot_a], around(row, j) * 8 + col, 3, rsem.at[4])
+            send(ph_b.at[slot_b], ph_b.at[slot_b], row * 8 + around(col, j), 11, rsem.at[5])
+            return 0
+
+        lax.fori_loop(0, 7, go, 0)
+
+    pass_on(me, turned)
+
+    def relay(i, _):
+        j = 6 - i
+        wait(asem.at[0, j], ph_a, 1)
+        wait(asem.at[1, j], ph_b, 1)
+        from_col = lax.rem(col - offset(j) + 8, 8)
+        from_row = lax.rem(row - offset(j) + 8, 8)
+        pass_on(row * 8 + from_col, col * 8 + from_row)
+        return 0
+
+    lax.fori_loop(0, 7, relay, 0)
 
     mrecv[me] = msend[me]
     to_all(4, lambda p: msend.at[p], mrecv, lambda g: rsem.at[6])
@@ -321,11 +339,29 @@
 
     wait(rsem.at[6], mrecv, 63)
     margin = join(jnp.sum(mrecv[...].astype(F32), axis=0), me)
-    mown[...] = halve(margin, me)
-    mall[me] = mown[...]
-    to_all(5, lambda p: mown, mall, lambda g: rsem.at[7])
+    whole = halve(margin, me)
+    m_a[me] = whole[:, :256]
+    m_b[turned] = whole[:, 256:]
+
+    def margin_one(j, _):
+        send(m_a.at[me], m_a.at[me], row * 8 + around(col, j), 5, rsem.at[2])
+        send(m_b.at[turned], m_b.at[turned], around(row, j) * 8 + col, 12, rsem.at[3])
+        return 0
+
+    lax.fori_loop(0, 7, margin_one, 0)
+
+    def margin_all(j, _):
+        part_a = m_a.at[pl.ds(row * 8, 8)]
+        part_b = m_b.at[pl.ds(col * 8, 8)]
+        send(part_a, part_a, around(row, j) * 8 + col, 13, rsem.at[7])
+        send(part_b, part_b, row * 8 + around(col, j), 14, rsem.at[9])
+        return 0
 
     for o in range(OWNERS):
+        if o == 3:
+            wait(rsem.at[2], m_a, 7)
+            wait(rsem.at[3], m_b, 7)
+            lax.fori_loop(0, 7, margin_all, 0)
         ph_re, ph_im = phase(2 * o), phase(2 * o + 1)
         solved = jnp.dot(
             firstt[...], mid[:, o * 512 : (o + 1) * 512], preferred_element_type=F32
@@ -355,7 +391,15 @@
     vrecv[me] = vsend[me]
     to_all(6, lambda p: vsend.at[p], vrecv, lambda g: gsem.at[0, g])
 
-    wait(rsem.at[7], mall, 63)
+    wait(rsem.at[7], m_a, 56)
+    wait(rsem.at[9], m_b, 56)
+
+    def gathered(i, _):
+        mall[i, :, 0:256] = m_a[i]
+        mall[i, :, 256:512] = m_b[lax.rem(i, 8) * 8 + i // 8]
+        return 0
+
+    lax.fori_loop(0, 64, gathered, 0)
     mt[...] = widen(join(mall[...].astype(F32).reshape(256, 512), 0))
 
     def take_values(g, count):
@@ -376,7 +420,14 @@
     )
     cown[...] = coeff.astype(BF16)
     call[me] = cown[...]
-    to_all(8, lambda p: cown, call, lambda g: gsem.at[1, g])
+
+    def coefficients_out(i, _):
+        step = 62 - i
+        peer = around(row, step // 8) * 8 + around(col, step % 8)
+        send(cown, call.at[me], peer, 8, gsem.at[1, step // 8])
+        return 0
+
+    lax.fori_loop(0, 63, coefficients_out, 0)
 
     def take_coefficients(g, count):
         source = lax.rem(row - offset(g) + 8, 8)
@@ -388,7 +439,7 @@
         rsend[pl.ds(base, 8)] = (own - correction).reshape(8, 8, 512).astype(BF16)
         to_row(9, base, count, lambda p: rsend.at[p], rrecv, gsem.at[2, g])
 
-    by_rows(take_coefficients)
+    by_near_rows(take_coefficients)
     rrecv[me] = rsend[me]
 
     def take_residuals(g, count):
@@ -401,17 +452,17 @@
         cells = pl.ds(base, 4096)
         pltpu.make_async_copy(result.at[:, :, cells], out.at[:, :, cells], fsem).start()
 
-    by_rows(take_residuals)
+    by_near_rows(take_residuals)
     pltpu.make_async_copy(result, out, fsem).wait()
 
     for n, ref in (
-        (0, osend), (4, msend), (5, mall), (6, vsend), (7, psend), (8, call), (9, rsend)
+        (0, osend), (4, msend), (6, vsend), (7, psend), (8, call), (9, rsend)
     ):
         wait(ssem.at[n], ref, 63)
     wait(ssem.at[1], sh, 7)
-    for n, ref in ((2, ph_a), (10, ph_b)):
+    for n, ref in ((2, ph_a), (10, ph_b), (5, m_a), (12, m_b)):
         wait(ssem.at[n], ref, 7)
-    for n, ref in ((3, ph_a), (11, ph_b)):
+    for n, ref in ((3, ph_a), (11, ph_b), (13, m_a), (14, m_b)):
         wait(ssem.at[n], ref, 56)
 
 
@@ -444,7 +495,8 @@
             pltpu.VMEM((64, 8, 256), BF16),
             pltpu.VMEM(thin, BF16),
             pltpu.VMEM(thin, BF16),
-            pltpu.VMEM((4, 512), BF16),
+            pltpu.VMEM((64, 4, 256), BF16),
+            pltpu.VMEM((64, 4, 256), BF16),
             pltpu.VMEM(thin, BF16),
             pltpu.VMEM((512, 512), F32),
             pltpu.VMEM((512, 512), BF16),
@@ -461,10 +513,11 @@
             pltpu.VMEM(slab, BF16),
             pltpu.VMEM((2, 4, GRID), BF16),
             pltpu.SemaphoreType.DMA((6,)),
-            pltpu.SemaphoreType.DMA((12,)),
-            pltpu.SemaphoreType.DMA((9,)),
+            pltpu.SemaphoreType.DMA((15,)),
+            pltpu.SemaphoreType.DMA((10,)),
             pltpu.SemaphoreType.DMA((3, 8)),
             pltpu.SemaphoreType.DMA,
+            pltpu.SemaphoreType.DMA((2, 7)),
         ],
         compiler_params=pltpu.CompilerParams(
             collective_id=0, has_side_effects=True, vmem_limit_bytes=60 << 20

time: 111 us -> 112 us (level)
  the two profiles are of different devices: /device:TPU:1 before, /device:TPU:12 now
where the time goes in v3:
time: 112 us
  Pallas kernels  110 us (98%)
  local copies, waits for them, and re-layouts  2.02 us (2%)
    pallas_call x1, Pallas kernels, body(): pl.pallas_call(kernel, out_shape=jax.ShapeDtypeStruct((2, 4, GRID), BF16)...  110 us

profile of v3, /device:TPU:12, one launch (start us, length us, event | category | flops | bytes accessed | tf_op | source)
XLA Modules:
  0.0 111.8 jit_solution(8345038662358759198)
XLA Ops:
  0.0 109.8 %exchange_residual.1 = bf16[2,4,32768]{2,1,0:T(4,128)(2,1)} custom-call(bf16[2,4,32768]{2,1,0:T(4,128)(2,1)} %bitcast.6, f32[256,128]{1,0:T(8,128)} %bitcast.7, f32[256,128]{1,0:T(8,128)} %bitcast.8, s32[4]{0:T(128)} %owners.1, s32[4,8]{1,0:T(4,128)} %bitcast.9, bf16[512,512]{1,0:T(8,128)(2,1)} %constant.6.clone.first_hbm, ...), custom_call_target="tpu_custom_call" | custom-call | tf_op jit(solution)/shard_map/exchange_residual/pallas_call | solution.py:475
  109.8 2.0 %copy.10 = bf16[1,2,4,32768]{3,2,1,0:T(4,128)(2,1)} copy(bf16[1,2,4,32768]{3,2,1,0:T(4,128)(2,1)} %bitcast.5) | data formatting | bytes 1048576

commit v4 on v3

--- a/solution.py
+++ b/solution.py
@@ -21,7 +21,7 @@
 
 def tables():
     spot = np.arange(256)
-    plane = (spot % 64) * 4 + spot // 64
+    plane = (spot // 32 * 8 + spot % 8) * 4 + spot // 8 % 4
     cell_x, cell_y = plane // 8, plane % 8
     freq_x, freq_y = spot % 32, spot // 32
     outer = np.exp(
@@ -51,7 +51,7 @@
     out,
     x, pot, kern, first, firstt, second, spread, bands, kgrid,
     osend, orecv, xs, sh, ph_a, ph_b, msend, mrecv, m_a, m_b, mall, mt,
-    dens, mid, acc, vsend, vrecv, ys, psend, precv, cown, call, rsend, rrecv, result,
+    dens, mid, acc, phases, vsend, vrecv, ys, psend, precv, cown, call, rsend, rrecv, result,
     csem, ssem, rsem, gsem, fsem, asem,
 ):
     me = lax.axis_index("band")
@@ -147,20 +147,14 @@
         lax.fori_loop(0, 7, run, 0)
         step(7, 7)
 
-    def by_near_rows(step):
-        def run(i, _):
-            step(6 - i, 8)
-            return 0
-
-        step(7, 7)
-        lax.fori_loop(0, 7, run, 0)
-
     orecv[me] = osend[me]
     to_all(0, lambda p: osend.at[p], orecv, lambda g: rsem.at[0])
 
     for f in range(8):
-        for i in range(4):
-            bands[f, i * 64 : (i + 1) * 64, :] = spread[pl.ds(i * 512 + f, 64, stride=8), :]
+        for r in range(8):
+            for i in range(4):
+                at = r * 32 + i * 8
+                bands[f, at : at + 8, :] = spread[pl.ds(i * 512 + r * 64 + f, 8, stride=8), :]
     loads[2].wait()
     lane128 = lax.broadcasted_iota(jnp.int32, (32, 128), 1)
     for h in range(8):
@@ -287,17 +281,20 @@
         at = slice((i % 2) * 128, (i % 2 + 1) * 128)
         spread[i * 512 : (i + 1) * 512, :] = source[:, :, at].astype(F32).reshape(512, 128)
 
-    def phase(f):
-        parts = [spread[pl.ds(i * 512 + f, 64, stride=8), :] for i in range(2)]
-        for i in range(2, 4):
-            for r in range(8):
-                parts.append(spread[pl.ds(i * 512 + r * 8 + f, 8, stride=64), :])
-        return jnp.concatenate(parts, axis=0)
+    for f in range(8):
+        for r in range(8):
+            for i in range(4):
+                at = r * 32 + i * 8
+                if i < 2:
+                    part = spread[pl.ds(i * 512 + r * 64 + f, 8, stride=8), :]
+                else:
+                    part = spread[pl.ds(i * 512 + r * 8 + f, 8, stride=64), :]
+                phases[f, at : at + 8, :] = part
 
     for load in loads[3:]:
         load.wait()
     for o in range(OWNERS):
-        ph_re, ph_im = phase(2 * o), phase(2 * o + 1)
+        ph_re, ph_im = phases[2 * o], phases[2 * o + 1]
         for b in range(4):
             b_re, b_im = bands[b], bands[4 + b]
             at = b * 128
@@ -357,39 +354,63 @@
         send(part_b, part_b, row * 8 + around(col, j), 14, rsem.at[9])
         return 0
 
-    for o in range(OWNERS):
-        if o == 3:
-            wait(rsem.at[2], m_a, 7)
-            wait(rsem.at[3], m_b, 7)
-            lax.fori_loop(0, 7, margin_all, 0)
-        ph_re, ph_im = phase(2 * o), phase(2 * o + 1)
-        solved = jnp.dot(
-            firstt[...], mid[:, o * 512 : (o + 1) * 512], preferred_element_type=F32
+    loads[1].wait()
+
+    def values_out(g, count):
+        r = around(row, g)
+        base = pl.multiple_of(r * 32, 32)
+        local = jnp.concatenate(
+            [pot[pl.ds(r * 32 + i, 8, stride=4), :] for i in range(4)], axis=0
         )
-        for b in range(4):
-            s_re = solved[0:256, b * 128 : (b + 1) * 128]
-            s_im = solved[256:512, b * 128 : (b + 1) * 128]
-            t_re = ph_re * s_re - ph_im * s_im
-            t_im = ph_re * s_im + ph_im * s_re
-            if o:
-                t_re = acc[b] + t_re
-                t_im = acc[4 + b] + t_im
-            acc[b] = t_re
-            acc[4 + b] = t_im
-
-    loads[1].wait()
-    for i in range(4):
-        local = pot[pl.ds(i, 64, stride=4), :]
-        rows = slice(i * 64, (i + 1) * 64)
+        slot = pl.multiple_of(lax.rem(g, 4) * 32, 32)
         for f in range(8):
-            spread[pl.ds(i * 512 + f, 64, stride=8), :] = (
-                local * bands[f, rows, :] + SHARE * acc[f, rows, :]
+            value = local * bands[f, pl.ds(base, 32), :] + SHARE * acc[f, pl.ds(slot, 32), :]
+            for i in range(4):
+                spread[pl.ds(i * 512 + r * 64 + f, 8, stride=8), :] = value[i * 8 : (i + 1) * 8]
+        first_slab = pl.multiple_of(r * 8, 8)
+        for i in range(4):
+            part = spread[pl.ds(pl.multiple_of(i * 512 + r * 64, 64), 64), :]
+            vsend[pl.ds(first_slab, 8), :, i * 128 : (i + 1) * 128] = part.reshape(
+                8, 8, 128
+            ).astype(BF16)
+        to_row(6, first_slab, count, lambda p: vsend.at[p], vrecv, gsem.at[0, g])
+
+    for half in range(2):
+        starts = [
+            pl.multiple_of(around(row, 4 * half + q) * 32, 32) for q in range(4)
+        ]
+
+        def chosen(ref, at=0):
+            return jnp.concatenate([ref[pl.ds(at + r, 32), :] for r in starts], axis=0)
+
+        lines = jnp.concatenate([chosen(firstt), chosen(firstt, 256)], axis=0)
+        for o in range(OWNERS):
+            if half == 0 and o == 3:
+                wait(rsem.at[2], m_a, 7)
+                wait(rsem.at[3], m_b, 7)
+                lax.fori_loop(0, 7, margin_all, 0)
+            ph_re, ph_im = chosen(phases.at[2 * o]), chosen(phases.at[2 * o + 1])
+            solved = jnp.dot(
+                lines, mid[:, o * 512 : (o + 1) * 512], preferred_element_type=F32
             )
-    for i in range(4):
-        part = spread[i * 512 : (i + 1) * 512, :].reshape(64, 8, 128)
-        vsend[:, :, i * 128 : (i + 1) * 128] = part.astype(BF16)
+            for b in range(4):
+                s_re = solved[0:128, b * 128 : (b + 1) * 128]
+                s_im = solved[128:256, b * 128 : (b + 1) * 128]
+                t_re = ph_re * s_re - ph_im * s_im
+                t_im = ph_re * s_im + ph_im * s_re
+                if o:
+                    t_re = acc[b] + t_re
+                    t_im = acc[4 + b] + t_im
+                acc[b] = t_re
+                acc[4 + b] = t_im
+
+        def run(g, _):
+            values_out(g, 8)
+            return 0
+
+        lax.fori_loop(4 * half, 4 + 3 * half, run, 0)
+    values_out(7, 7)
     vrecv[me] = vsend[me]
-    to_all(6, lambda p: vsend.at[p], vrecv, lambda g: gsem.at[0, g])
 
     wait(rsem.at[7], m_a, 56)
     wait(rsem.at[9], m_b, 56)
@@ -420,14 +441,7 @@
     )
     cown[...] = coeff.astype(BF16)
     call[me] = cown[...]
-
-    def coefficients_out(i, _):
-        step = 62 - i
-        peer = around(row, step // 8) * 8 + around(col, step % 8)
-        send(cown, call.at[me], peer, 8, gsem.at[1, step // 8])
-        return 0
-
-    lax.fori_loop(0, 63, coefficients_out, 0)
+    to_all(8, lambda p: cown, call, lambda g: gsem.at[1, g])
 
     def take_coefficients(g, count):
         source = lax.rem(row - offset(g) + 8, 8)
@@ -439,7 +453,7 @@
         rsend[pl.ds(base, 8)] = (own - correction).reshape(8, 8, 512).astype(BF16)
         to_row(9, base, count, lambda p: rsend.at[p], rrecv, gsem.at[2, g])
 
-    by_near_rows(take_coefficients)
+    by_rows(take_coefficients)
     rrecv[me] = rsend[me]
 
     def take_residuals(g, count):
@@ -452,7 +466,7 @@
         cells = pl.ds(base, 4096)
         pltpu.make_async_copy(result.at[:, :, cells], out.at[:, :, cells], fsem).start()
 
-    by_near_rows(take_residuals)
+    by_rows(take_residuals)
     pltpu.make_async_copy(result, out, fsem).wait()
 
     for n, ref in (
@@ -501,6 +515,7 @@
             pltpu.VMEM((512, 512), F32),
             pltpu.VMEM((512, 512), BF16),
             pltpu.VMEM((512, 2048), BF16),
+            pltpu.VMEM((8, 128, 128), F32),
             pltpu.VMEM((8, 256, 128), F32),
             pltpu.VMEM(slab, BF16),
             pltpu.VMEM(slab, BF16),

time: 112 us -> 111 us (level)
  the two profiles are of different devices: /device:TPU:12 before, /device:TPU:1 now
where the time goes in v4:
time: 111 us
  Pallas kernels  109 us (98%)
  local copies, waits for them, and re-layouts  2.02 us (2%)
    pallas_call x1, Pallas kernels, body(): pl.pallas_call(kernel, out_shape=jax.ShapeDtypeStruct((2, 4, GRID), BF16)...  109 us

profile of v4, /device:TPU:1, one launch (start us, length us, event | category | flops | bytes accessed | tf_op | source)
XLA Modules:
  0.0 110.8 jit_solution(11154137760048095486)
XLA Ops:
  0.0 108.8 %exchange_residual.1 = bf16[2,4,32768]{2,1,0:T(4,128)(2,1)} custom-call(bf16[2,4,32768]{2,1,0:T(4,128)(2,1)} %bitcast.6, f32[256,128]{1,0:T(8,128)} %bitcast.7, f32[256,128]{1,0:T(8,128)} %bitcast.8, s32[4]{0:T(128)} %owners.1, s32[4,8]{1,0:T(4,128)} %bitcast.9, bf16[512,512]{1,0:T(8,128)(2,1)} %constant.6.clone.first_hbm, ...), custom_call_target="tpu_custom_call" | custom-call | tf_op jit(solution)/shard_map/exchange_residual/pallas_call | solution.py:489
  108.8 2.0 %copy.10 = bf16[1,2,4,32768]{3,2,1,0:T(4,128)(2,1)} copy(bf16[1,2,4,32768]{3,2,1,0:T(4,128)(2,1)} %bitcast.5) | data formatting | bytes 1048576

commit v5 on v4

--- a/solution.py
+++ b/solution.py
@@ -79,12 +79,24 @@
 
     barrier = pltpu.get_barrier_semaphore()
 
-    def greet(step, _):
-        peer = around(row, step // 8) * 8 + around(col, step % 8)
-        pl.semaphore_signal(barrier, inc=1, device_id={"band": peer}, device_id_type=MESH)
-        return 0
-
-    lax.fori_loop(0, 63, greet, 0)
+    rows = [around(row, j) for j in range(8)]
+    cols = [around(col, j) for j in range(8)]
+
+    def over_rows(step):
+        def run(g, _):
+            step(g, around(row, g) * 8, 8)
+            return 0
+
+        lax.fori_loop(0, 7, run, 0)
+        step(7, row * 8, 7)
+
+    def greet(g, base, count):
+        for j in range(count):
+            pl.semaphore_signal(
+                barrier, inc=1, device_id={"band": base + cols[j]}, device_id_type=MESH
+            )
+
+    over_rows(greet)
 
     def greet_kpt(step, _):
         pl.semaphore_signal(
@@ -106,7 +118,7 @@
         osend[d] = wide.astype(BF16)
         return 0
 
-    lax.fori_loop(0, 64, pack, 0)
+    lax.fori_loop(0, 64, pack, 0, unroll=4)
     pl.semaphore_wait(barrier, 70)
 
     def send(source, target, peer, n, arrival):
@@ -124,20 +136,12 @@
         pltpu.make_async_copy(part, part, sem).wait()
 
     def to_all(n, source, dst, arrival):
-        def go(step, _):
-            peer = around(row, step // 8) * 8 + around(col, step % 8)
-            send(source(peer), dst.at[me], peer, n, arrival(step // 8))
-            return 0
-
-        lax.fori_loop(0, 63, go, 0)
+        over_rows(lambda g, base, count: to_row(n, base, count, source, dst, arrival(g)))
 
     def to_row(n, base, count, source, dst, arrival):
-        def go(j, _):
-            peer = base + around(col, j)
+        for j in range(count):
+            peer = base + cols[j]
             send(source(peer), dst.at[me], peer, n, arrival)
-            return 0
-
-        lax.fori_loop(0, count, go, 0)
 
     def by_rows(step):
         def run(g, _):
@@ -195,12 +199,12 @@
     lax.fori_loop(1, 8, kpt_go, 0)
 
     def fold(gram):
-        rows = gram.shape[0]
+        height = gram.shape[0]
         half = lax.broadcasted_iota(jnp.int32, gram.shape, 1) % 8 < 4
-        low = pltpu.roll(gram, rows - 4, 0)
+        low = pltpu.roll(gram, height - 4, 0)
         swapped = jnp.where(half, pltpu.roll(low, 508, 1), -pltpu.roll(low, 4, 1))
-        sums = ((gram + swapped) * (1.0 / GRID)).reshape(rows // 8, 8, 512)[:, :4, :]
-        return sums.reshape(rows // 2, 512)
+        sums = ((gram + swapped) * (1.0 / GRID)).reshape(height // 8, 8, 512)[:, :4, :]
+        return sums.reshape(height // 2, 512)
 
     def widen(flat):
         half = lax.broadcasted_iota(jnp.int32, flat.shape, 1) % 8 < 4
@@ -243,20 +247,14 @@
     ph_a[me] = got[:, :256].astype(BF16)
     ph_b[turned] = got[:, 256:].astype(BF16)
 
-    def spread_one(j, _):
-        send(ph_a.at[me], ph_a.at[me], row * 8 + around(col, j), 2, asem.at[0, j])
-        send(ph_b.at[turned], ph_b.at[turned], around(row, j) * 8 + col, 10, asem.at[1, j])
-        return 0
-
-    lax.fori_loop(0, 7, spread_one, 0)
+    for j in range(7):
+        send(ph_a.at[me], ph_a.at[me], row * 8 + cols[j], 2, asem.at[0, j])
+        send(ph_b.at[turned], ph_b.at[turned], rows[j] * 8 + col, 10, asem.at[1, j])
 
     def pass_on(slot_a, slot_b):
-        def go(j, _):
-            send(ph_a.at[slot_a], ph_a.at[slot_a], around(row, j) * 8 + col, 3, rsem.at[4])
-            send(ph_b.at[slot_b], ph_b.at[slot_b], row * 8 + around(col, j), 11, rsem.at[5])
-            return 0
-
-        lax.fori_loop(0, 7, go, 0)
+        for j in range(7):
+            send(ph_a.at[slot_a], ph_a.at[slot_a], rows[j] * 8 + col, 3, rsem.at[4])
+            send(ph_b.at[slot_b], ph_b.at[slot_b], row * 8 + cols[j], 11, rsem.at[5])
 
     pass_on(me, turned)
 
@@ -340,19 +338,16 @@
     m_a[me] = whole[:, :256]
     m_b[turned] = whole[:, 256:]
 
-    def margin_one(j, _):
-        send(m_a.at[me], m_a.at[me], row * 8 + around(col, j), 5, rsem.at[2])
-        send(m_b.at[turned], m_b.at[turned], around(row, j) * 8 + col, 12, rsem.at[3])
-        return 0
-
-    lax.fori_loop(0, 7, margin_one, 0)
-
-    def margin_all(j, _):
+    for j in range(7):
+        send(m_a.at[me], m_a.at[me], row * 8 + cols[j], 5, rsem.at[2])
+        send(m_b.at[turned], m_b.at[turned], rows[j] * 8 + col, 12, rsem.at[3])
+
+    def margin_all():
         part_a = m_a.at[pl.ds(row * 8, 8)]
         part_b = m_b.at[pl.ds(col * 8, 8)]
-        send(part_a, part_a, around(row, j) * 8 + col, 13, rsem.at[7])
-        send(part_b, part_b, row * 8 + around(col, j), 14, rsem.at[9])
-        return 0
+        for j in range(7):
+            send(part_a, part_a, rows[j] * 8 + col, 13, rsem.at[7])
+            send(part_b, part_b, row * 8 + cols[j], 14, rsem.at[9])
 
     loads[1].wait()
 
@@ -388,7 +383,7 @@
             if half == 0 and o == 3:
                 wait(rsem.at[2], m_a, 7)
                 wait(rsem.at[3], m_b, 7)
-                lax.fori_loop(0, 7, margin_all, 0)
+                margin_all()
             ph_re, ph_im = chosen(phases.at[2 * o]), chosen(phases.at[2 * o + 1])
             solved = jnp.dot(
                 lines, mid[:, o * 512 : (o + 1) * 512], preferred_element_type=F32

time: 111 us -> 107 us (0.964)
  the two profiles are of different devices: /device:TPU:1 before, /device:TPU:2 now
where the time goes in v5:
time: 107 us
  Pallas kernels  105 us (98%)
  local copies, waits for them, and re-layouts  2.02 us (2%)
    pallas_call x1, Pallas kernels, body(): pl.pallas_call(kernel, out_shape=jax.ShapeDtypeStruct((2, 4, GRID), BF16)...  105 us

profile of v5, /device:TPU:2, one launch (start us, length us, event | category | flops | bytes accessed | tf_op | source)
XLA Modules:
  0.0 107.2 jit_solution(798900165140252082)
XLA Ops:
  0.0 105.2 %exchange_residual.1 = bf16[2,4,32768]{2,1,0:T(4,128)(2,1)} custom-call(bf16[2,4,32768]{2,1,0:T(4,128)(2,1)} %bitcast.6, f32[256,128]{1,0:T(8,128)} %bitcast.7, f32[256,128]{1,0:T(8,128)} %bitcast.8, s32[4]{0:T(128)} %owners.1, s32[4,8]{1,0:T(4,128)} %bitcast.9, bf16[512,512]{1,0:T(8,128)(2,1)} %constant.6.clone.first_hbm, ...), custom_call_target="tpu_custom_call" | custom-call | tf_op jit(solution)/shard_map/exchange_residual/pallas_call | solution.py:484
  105.2 2.0 %copy.10 = bf16[1,2,4,32768]{3,2,1,0:T(4,128)(2,1)} copy(bf16[1,2,4,32768]{3,2,1,0:T(4,128)(2,1)} %bitcast.5) | data formatting | bytes 1048576
